TPU v7x, 256 devices: a whole 4x4x8 slice. The times are simulated.
256 devices in a mesh: ctx: 32 (over x, z), grp: 8 (over y, core).
Axes of the slice: x: 4, y: 4, z: 8, core: 2. Of those that a mesh axis runs over, the one named last changes fastest.
Arguments:
- out_grad: bfloat16 [16384, 2048], P('ctx', 'grp'), may hold values from -6 to 6
- filter_mats: bfloat16 [16, 2048, 2048], P('grp', 'ctx'), may hold values from -0.125 to 0.125
- coeffs: float32 [16, 80], replicated, may hold values from -0.15625 to 0.15625
- pole_rates: float32 [80], replicated, may hold values from 1.2207031e-06 to 0.03
Outputs:
- in_grad: bfloat16 [16384, 2048], P('ctx', 'grp')
All inputs are finite; a program needn't handle non-finite values.
Results may differ from a plain program's by a relative error of at most 0.001.
Values may be sent and summed in bfloat16 or wider, within the bound.
A program may use at most 128 MiB of HBM per device.

v0:
```python
import jax
import jax.numpy as jnp
from jax import lax
from jax.sharding import PartitionSpec as P

exact_prec = lax.Precision.HIGHEST


def entering(array, axis, combine, identity):
    count, here = (lax.axis_size(axis), lax.axis_index(axis))
    everything = jax.tree.map(lambda part: lax.all_gather(part, axis), array)
    start = jax.tree.map(
        lambda part, zero: jnp.broadcast_to(jnp.asarray(zero, part.dtype), part.shape),
        array,
        identity,
    )

    def step(k, before):
        at = count - 1 - k
        reached = at > here
        new = combine(before, jax.tree.map(lambda part: part[at], everything))
        return jax.tree.map(lambda a, b: jnp.where(reached, a, b), new, before)

    return lax.fori_loop(0, count, step, start)


def merge_suffix(earlier, latter):
    carried_e, factor_e = earlier
    carried_l, factor_l = latter
    return (carried_l + factor_l * carried_e, factor_l * factor_e)


def per_device(out_grad, filter_mats, coeffs, pole_rates):
    full_grad = lax.all_gather(out_grad, "grp", axis=1, tiled=True)
    length = full_grad.shape[0]
    col_width = out_grad.shape[1]
    poles = pole_rates.shape[0]
    positions = jnp.arange(length, dtype=jnp.float32)
    pole_gains = jnp.sqrt(-jnp.expm1(-2.0 * pole_rates))
    middle = float(length // 2)
    rising = jnp.exp(-(positions[:, None] - middle) * pole_rates[None, :])
    falling = jnp.exp((positions[:, None] - middle) * pole_rates[None, :])
    causal = positions[:, None] >= positions[None, :]
    decay_pos = jnp.exp(-positions[:, None] * pole_rates[None, :])
    edge_decay = pole_gains[None, :] * jnp.exp(-(length - positions)[:, None] * pole_rates[None, :])
    block_decay = jnp.exp(-length * pole_rates)[:, None]
    unit_factor = jnp.ones((poles, 1), jnp.float32)
    filters = filter_mats.shape[0]
    own_coeffs = lax.dynamic_slice_in_dim(coeffs, lax.axis_index("grp") * filters, filters, 0)
    kernel_mat = jnp.einsum(
        "tp,kp,sp->kts", rising, own_coeffs * pole_gains[None, :], falling, precision=exact_prec
    )
    kernel_mat = jnp.where(causal[None], kernel_mat, 0.0)
    weights = own_coeffs[:, :, None] * decay_pos.T[None]
    proj_grad = jnp.einsum(
        "tj,kij->kti",
        full_grad,
        lax.all_gather(filter_mats, "ctx", axis=1, tiled=True),
        preferred_element_type=jnp.float32,
    )
    near_part = jnp.einsum("kts,kti->si", kernel_mat, proj_grad, precision=exact_prec)
    pole_part = jnp.einsum("kpt,kti->pi", weights, proj_grad, precision=exact_prec)
    stacked = jnp.concatenate([near_part, pole_part], axis=0)
    near_sum = lax.psum_scatter(stacked[:length], "grp", scatter_dimension=1, tiled=True)
    pole_sum = lax.psum(stacked[length:], "grp")
    later_all = entering(
        (pole_sum, block_decay), "ctx", merge_suffix, (jnp.zeros_like(pole_sum), unit_factor)
    )[0]
    own_cols = lax.dynamic_slice_in_dim(later_all, lax.axis_index("grp") * col_width, col_width, 1)
    total = near_sum + jnp.dot(edge_decay, own_cols, precision=exact_prec)
    return total.astype(jnp.bfloat16)


def solution(mesh):
    placed = (P("ctx", "grp"), P("grp", "ctx", None), P(), P())
    return jax.shard_map(
        per_device, mesh=mesh, in_specs=placed, out_specs=P("ctx", "grp"), check_vma=False
    )
```

profile of v0, /device:TPU:0, one launch (start us, length us, event | category | flops | bytes accessed | tf_op | source)
XLA Modules:
  0.0 490.5 jit_solution(5679977234924721466)
XLA Ops:
  8.1 1.3 dynamic-slice
  12.2 27.7 %all-gather.7.cloned.1.call-done = bf16[512,2048]{1,0:T(8,128)(2,1)} async-done(((bf16[512,256]{1,0:T(8,128)(2,1)}), bf16[512,2048]{1,0:T(8,128)(2,1)}) %all-gather.7.cloned.1.call-update) | async-done | bytes 2097168 | tf_op jit(solution)/shard_map/all_gather | solution.py:34
  39.9 143.1 %all-gather.5.cloned.1.call-done = bf16[2,2048,2048]{2,1,0:T(8,128)(2,1)} async-done(((bf16[2,64,2048]{2,1,0:T(8,128)(2,1)}), bf16[2,2048,2048]{2,1,0:T(8,128)(2,1)}) %all-gather.5.cloned.1.call-update) | async-done | bytes 16777232 | tf_op jit(solution)/shard_map/all_gather | solution.py:58
  183.0 12.9 %fusion.11 = f32[2,2048,512]{2,1,0:T(8,128)S(1)} fusion(bf16[2,2048,2048]{2,1,0:T(8,128)(2,1)} %all-gather.5.cloned.1.call-done, bf16[512,2048]{1,0:T(8,128)(2,1)} %all-gather.7.cloned.1.call-done), kind=kOutput, calls=%fused_computation.9 | convolution fusion | flops 8589934592 | bytes 27262976 | tf_op jit(solution)/shard_map/tj,kij->kti/dot_general | solution.py:55
  195.9 3.3 copy-done
  199.2 9.1 %fusion.8 = f32[1,80,2048]{2,1,0:T(8,128)} fusion(f32[2,2048,512]{2,1,0:T(8,128)S(1)} %fusion.11, f32[80,512]{1,0:T(8,128)S(1)} %multiply_exponential_fusion, f32[2,80]{1,0:T(2,128)S(1)} %get-tuple-element.167), kind=kOutput, calls=%fused_computation.8 | convolution fusion | flops 2013347840 | bytes 9208448 | tf_op jit(solution)/shard_map/kpt,kti->pi/dot_general | solution.py:62
  208.3 63.9 %all-reduce.3.cloned.1.call-done = f32[1,80,2048]{2,1,0:T(8,128)} async-done(((f32[1,80,2048]{2,1,0:T(8,128)}), f32[1,80,2048]{2,1,0:T(8,128)}) %all-reduce.3.cloned.1.call-update) | async-done | bytes 655376 | tf_op jit(solution)/shard_map/psum | solution.py:65
  272.4 147.7 %all-reduce = f32[2560]{0:T(1024)S(1)} all-reduce(f32[2560]{0:T(1024)S(1)} %get-tuple-element.168), channel_id=2, replica_groups=mesh['ctx'=32,'grp'=8] {'ctx'}, use_global_device_ids=true, to_apply=%add | all-reduce | flops 2560 | bytes 20480
  420.7 1.9 fusion.17
  422.6 17.5 %fusion.5 = f32[512,2048]{1,0:T(8,128)} fusion(f32[2,2048,512]{2,1,0:T(8,128)} %copy-done, f32[2,512,512]{1,2,0:T(8,128)S(1)} %fusion.17, pred[512,512]{0,1:T(8,128)(4,1)S(1)} %iota_compare_fusion), kind=kOutput, calls=%fused_computation.7 | convolution fusion | flops 12885426176 | bytes 14942208 | tf_op jit(solution)/shard_map/kts,kti->si/dot_general | solution.py:61
  440.1 41.4 %while.16 = (s32[]{:T(128)}, f32[80,2048]{1,0:T(8,128)S(1)}, s32[]{:T(128)}, f32[32,80,2048]{2,1,0:T(8,128)}, f32[32,80,1]{1,2,0:T(1,128)S(1)}, /*index=5*/s32[]{:T(128)}, s32[]{:T(128)}, s32[]{:T(128)}, s32[]{:T(128)}) while((s32[]{:T(128)}, f32[80,2048]{1,0:T(8,128)S(1)}, s32[]{:T(128)}, f32[32,80,2048]{2,1,0:T(8,128)}, ...), condition=%wide.region_3.4_spmd.clone, body=%wide.region_2.3_spmd.clone.sunk | while | flops 655368 | bytes 1967215 | solution.py:24
  445.3 1.2 fusion.39
  446.6 1.3 fusion.39
  450.5 1.2 fusion.39
  451.8 1.3 fusion.39
  453.1 1.2 fusion.39
  454.4 1.2 fusion.39
  455.7 1.2 fusion.39
  458.3 1.2 fusion.39
  459.6 1.2 fusion.39
  460.8 1.2 fusion.39
  462.1 1.3 fusion.39
  463.4 1.2 fusion.39
  466.0 1.3 fusion.39
  467.3 1.3 fusion.39
  468.6 1.2 fusion.39
  469.9 1.2 fusion.39
  472.5 1.2 fusion.39
  473.8 1.2 fusion.39
  475.1 1.2 fusion.39
  479.0 1.2 fusion.39
  481.5 2.5 fusion.14
  (73 shorter events, 19.7 us)
Async XLA Ops:
  6.5 33.4 %all-gather.7.cloned.1.call-start = ((), (), s32[]{:S(2)}) async-start(), calls=%async_computation.2 | async-start | bytes 2359296 | tf_op jit(solution)/shard_map/all_gather | solution.py:34
  7.3 175.8 %all-gather.5.cloned.1.call-start = ((), (), s32[]{:S(2)}) async-start(), calls=%async_computation.1 | async-start | bytes 17301504 | tf_op jit(solution)/shard_map/all_gather | solution.py:58
  8.0 264.2 %all-reduce.3.cloned.1.call-start = ((), (), s32[]{:S(2)}) async-start(), calls=%async_computation.4 | async-start | bytes 1310720 | tf_op jit(solution)/shard_map/psum | solution.py:65
  195.9 3.3 copy-start
  195.9 224.5 %copy-start.1 = (f32[80]{0:T(128)S(1)}, f32[80]{0:T(128)}, u32[]{:S(2)}) copy-start(f32[80]{0:T(128)} %param.9) | copy-start | bytes 964
  208.3 231.8 %all-gather.9.cloned.1.call-start = ((), (), s32[]{:S(2)}) async-start(), calls=%async_computation.5 | async-start | bytes 21626880 | tf_op jit(solution)/shard_map/all_gather | solution.py:11
  272.2 209.3 %reduce-scatter.2.cloned.1.call-start = ((), (), s32[]{:S(2)}) async-start(), calls=%async_computation.3 | async-start | bytes 4718592 | tf_op jit(solution)/shard_map/reduce_scatter | solution.py:64
Sparse Core Ops, SparseCore 0:
  9.2 30.7 all-gather.6
  42.5 140.4 all-gather.4
  208.4 63.7 all-reduce.2
  274.6 161.0 all-gather.8
  440.2 35.2 reduce-scatter.1
where the time goes:
time: 492 us; the launch traced here: 491 us
  waiting for transfers between devices  236 us (48%)
  blocking collectives  148 us (30%)
  matrix products  43.8 us (9%)
  other arithmetic  42.5 us (9%)
  between operations  13.9 us (3%)
  local copies, waits for them, and re-layouts  4.96 us (1%)
    unnamed x1, blocking collectives  148 us
    all_gather x1, waiting for transfers between devices, per_device(): lax.all_gather(filter_mats, 'ctx', axis=1, tiled=True)  143 us
    psum x1, waiting for transfers between devices, per_device(): pole_sum = lax.psum(stacked[length:], 'grp')  63.9 us
    select_n x32, other arithmetic, step(): return jax.tree.map(lambda a, b: jnp.where(reached, a, b), new, before)  39.8 us
    all_gather x1, waiting for transfers between devices, per_device(): full_grad = lax.all_gather(out_grad, 'grp', axis=1, tiled=True)  27.7 us
    dot_general x1, matrix products, per_device(): jnp.einsum('kts,kti->si', kernel_mat, proj_grad, precision=exact_prec)  17.5 us
    dot_general x1, matrix products, per_device(): jnp.einsum('tj,kij->kti', full_grad, lax.all_gather(filter_mats, 'ctx', a...  12.9 us
  transfers between devices with their start and end apart: 5, of which 3 were waited for; matrix products, arithmetic and copies ran while one was open for 13% of the time, Pallas kernels for 0%

commit v1 on v0

--- a/solution.py
+++ b/solution.py
@@ -31,6 +31,12 @@
 
 
 def per_device(out_grad, filter_mats, coeffs, pole_rates):
+
+    def _list_keys(inputs, across):
+        clean = lax.all_gather(inputs, across)
+        y = jnp.sum(clean, 0)
+        return y
+
     full_grad = lax.all_gather(out_grad, "grp", axis=1, tiled=True)
     length = full_grad.shape[0]
     col_width = out_grad.shape[1]
@@ -62,7 +68,7 @@
     pole_part = jnp.einsum("kpt,kti->pi", weights, proj_grad, precision=exact_prec)
     stacked = jnp.concatenate([near_part, pole_part], axis=0)
     near_sum = lax.psum_scatter(stacked[:length], "grp", scatter_dimension=1, tiled=True)
-    pole_sum = lax.psum(stacked[length:], "grp")
+    pole_sum = _list_keys(stacked[length:], "grp")
     later_all = entering(
         (pole_sum, block_decay), "ctx", merge_suffix, (jnp.zeros_like(pole_sum), unit_factor)
     )[0]

time: 492 us -> 469 us (0.953)
  waiting for transfers between devices: 236 us -> 208 us
    psum x1 -> x0, waiting for transfers between devices: 63.9 us -> none  [per_device(): pole_sum = lax.psum(stacked[length:], 'grp')]
    all_gather x0 -> x1, waiting for transfers between devices: none -> 36.2 us  [_list_keys(): clean = lax.all_gather(inputs, across)]
  transfers between devices with their start and end apart: 5 -> 5, of which waited for: 3 -> 3; matrix products, arithmetic and copies ran while one was open for 13% -> 14% of each run, Pallas kernels for 0% -> 0%
where the time goes in v1:
time: 469 us; the launch traced here: 466 us
  waiting for transfers between devices  208 us (44%)
  blocking collectives  147 us (31%)
  other arithmetic  46.3 us (10%)
  matrix products  43.7 us (9%)
  between operations  13.9 us (3%)
  local copies, waits for them, and re-layouts  4.97 us (1%)
    unnamed x1, blocking collectives  147 us
    all_gather x1, waiting for transfers between devices, per_device(): lax.all_gather(filter_mats, 'ctx', axis=1, tiled=True)  143 us
    select_n x32, other arithmetic, step(): return jax.tree.map(lambda a, b: jnp.where(reached, a, b), new, before)  39.8 us
    all_gather x1, waiting for transfers between devices, _list_keys(): clean = lax.all_gather(inputs, across)  36.2 us
    all_gather x1, waiting for transfers between devices, per_device(): full_grad = lax.all_gather(out_grad, 'grp', axis=1, tiled=True)  27.7 us
    dot_general x1, matrix products, per_device(): jnp.einsum('kts,kti->si', kernel_mat, proj_grad, precision=exact_prec)  17.4 us
    dot_general x1, matrix products, per_device(): jnp.einsum('tj,kij->kti', full_grad, lax.all_gather(filter_mats, 'ctx', a...  12.9 us
  transfers between devices with their start and end apart: 5, of which 3 were waited for; matrix products, arithmetic and copies ran while one was open for 14% of the time, Pallas kernels for 0%

profile of v1, /device:TPU:0, one launch (start us, length us, event | category | flops | bytes accessed | tf_op | source)
XLA Modules:
  0.0 466.4 jit_solution(10913260917682523133)
XLA Ops:
  8.1 1.3 dynamic-slice
  12.2 27.7 %all-gather.10.cloned.1.call-done = bf16[512,2048]{1,0:T(8,128)(2,1)} async-done(((bf16[512,256]{1,0:T(8,128)(2,1)}), bf16[512,2048]{1,0:T(8,128)(2,1)}) %all-gather.10.cloned.1.call-update) | async-done | bytes 2097168 | tf_op jit(solution)/shard_map/all_gather | solution.py:40
  39.9 143.1 %all-gather.8.cloned.1.call-done = bf16[2,2048,2048]{2,1,0:T(8,128)(2,1)} async-done(((bf16[2,64,2048]{2,1,0:T(8,128)(2,1)}), bf16[2,2048,2048]{2,1,0:T(8,128)(2,1)}) %all-gather.8.cloned.1.call-update) | async-done | bytes 16777232 | tf_op jit(solution)/shard_map/all_gather | solution.py:64
  183.0 12.9 %fusion.11 = f32[2,2048,512]{2,1,0:T(8,128)S(1)} fusion(bf16[2,2048,2048]{2,1,0:T(8,128)(2,1)} %all-gather.8.cloned.1.call-done, bf16[512,2048]{1,0:T(8,128)(2,1)} %all-gather.10.cloned.1.call-done), kind=kOutput, calls=%fused_computation.9 | convolution fusion | flops 8589934592 | bytes 27262976 | tf_op jit(solution)/shard_map/tj,kij->kti/dot_general | solution.py:61
  195.9 3.3 copy-done
  199.2 9.1 %fusion.8 = f32[80,2048]{1,0:T(8,128)} fusion(f32[2,2048,512]{2,1,0:T(8,128)S(1)} %fusion.11, f32[80,512]{1,0:T(8,128)S(1)} %multiply_exponential_fusion, f32[2,80]{1,0:T(2,128)S(1)} %get-tuple-element.167), kind=kOutput, calls=%fused_computation.8 | convolution fusion | flops 2013347840 | bytes 9208448 | tf_op jit(solution)/shard_map/kpt,kti->pi/dot_general | solution.py:68
  208.3 36.2 %all-gather.12.cloned.1.call-done = f32[640,2048]{1,0:T(8,128)} async-done(((f32[80,2048]{1,0:T(8,128)}), f32[640,2048]{1,0:T(8,128)}) %all-gather.12.cloned.1.call-update) | async-done | bytes 5242896 | tf_op jit(solution)/shard_map/all_gather | solution.py:36
  244.6 3.7 reduce_sum.9
  248.5 147.5 %all-reduce = f32[2560]{0:T(1024)S(1)} all-reduce(f32[2560]{0:T(1024)S(1)} %get-tuple-element.168), channel_id=4, replica_groups=mesh['ctx'=32,'grp'=8] {'ctx'}, use_global_device_ids=true, to_apply=%add | all-reduce | flops 2560 | bytes 20480
  396.6 1.9 fusion.17
  398.5 17.4 %fusion.5 = f32[512,2048]{1,0:T(8,128)} fusion(f32[2,2048,512]{2,1,0:T(8,128)} %copy-done, f32[2,512,512]{1,2,0:T(8,128)S(1)} %fusion.17, pred[512,512]{0,1:T(8,128)(4,1)S(1)} %iota_compare_fusion), kind=kOutput, calls=%fused_computation.7 | convolution fusion | flops 12885426176 | bytes 14942208 | tf_op jit(solution)/shard_map/kts,kti->si/dot_general | solution.py:67
  416.0 41.4 %while.16 = (s32[]{:T(128)}, f32[80,2048]{1,0:T(8,128)S(1)}, s32[]{:T(128)}, f32[32,80,2048]{2,1,0:T(8,128)}, f32[32,80,1]{1,2,0:T(1,128)S(1)}, /*index=5*/s32[]{:T(128)}, s32[]{:T(128)}, s32[]{:T(128)}, s32[]{:T(128)}) while((s32[]{:T(128)}, f32[80,2048]{1,0:T(8,128)S(1)}, s32[]{:T(128)}, f32[32,80,2048]{2,1,0:T(8,128)}, ...), condition=%wide.region_3.4_spmd.clone, body=%wide.region_2.3_spmd.clone.sunk | while | flops 655368 | bytes 1967215 | solution.py:24
  421.2 1.3 fusion.39
  423.8 1.2 fusion.39
  425.1 1.2 fusion.39
  426.4 1.2 fusion.39
  427.7 1.2 fusion.39
  429.0 1.3 fusion.39
  430.3 1.3 fusion.39
  432.9 1.2 fusion.39
  434.2 1.3 fusion.39
  435.5 1.3 fusion.39
  436.8 1.2 fusion.39
  438.1 1.2 fusion.39
  440.6 1.3 fusion.39
  441.9 1.2 fusion.39
  443.2 1.2 fusion.39
  444.5 1.3 fusion.39
  448.4 1.2 fusion.39
  449.7 1.2 fusion.39
  452.3 1.2 fusion.39
  457.4 2.5 fusion.14
  (74 shorter events, 20.9 us)
Async XLA Ops:
  6.5 33.4 %all-gather.10.cloned.1.call-start = ((), (), s32[]{:S(2)}) async-start(), calls=%async_computation.2 | async-start | bytes 2359296 | tf_op jit(solution)/shard_map/all_gather | solution.py:40
  7.3 175.8 %all-gather.8.cloned.1.call-start = ((), (), s32[]{:S(2)}) async-start(), calls=%async_computation.1 | async-start | bytes 17301504 | tf_op jit(solution)/shard_map/all_gather | solution.py:64
  8.0 236.6 %all-gather.12.cloned.1.call-start = ((), (), s32[]{:S(2)}) async-start(), calls=%async_computation.4 | async-start | bytes 5898240 | tf_op jit(solution)/shard_map/all_gather | solution.py:36
  195.9 3.3 copy-start
  199.2 197.2 %copy-start.1 = (f32[80]{0:T(128)S(1)}, f32[80]{0:T(128)}, u32[]{:S(2)}) copy-start(f32[80]{0:T(128)} %param.9) | copy-start | bytes 964
  208.3 207.7 %all-gather.14.cloned.1.call-start = ((), (), s32[]{:S(2)}) async-start(), calls=%async_computation.5 | async-start | bytes 21626880 | tf_op jit(solution)/shard_map/all_gather | solution.py:11
  248.3 209.1 %reduce-scatter.2.cloned.1.call-start = ((), (), s32[]{:S(2)}) async-start(), calls=%async_computation.3 | async-start | bytes 4718592 | tf_op jit(solution)/shard_map/reduce_scatter | solution.py:70
Sparse Core Ops, SparseCore 0:
  9.2 30.7 all-gather.9
  42.5 140.4 all-gather.7
  208.4 36.1 all-gather.11
  248.4 161.9 all-gather.13
  416.1 34.2 reduce-scatter.1

commit v2 on v0

--- a/solution.py
+++ b/solution.py
@@ -1,9 +1,20 @@
+import functools
 import jax
 import jax.numpy as jnp
 from jax import lax
 from jax.sharding import PartitionSpec as P
 
 exact_prec = lax.Precision.HIGHEST
+
+
+def link_the_slabs(field_in, array_axis):
+    return jnp.concatenate(
+        jax.lax.all_to_all(jnp.stack([field_in] * jax.lax.axis_size("grp")), "grp", 0, 0),
+        axis=array_axis,
+    )
+
+
+connect_forms_here = functools.partial(link_the_slabs, array_axis=1)
 
 
 def entering(array, axis, combine, identity):
@@ -31,7 +42,7 @@
 
 
 def per_device(out_grad, filter_mats, coeffs, pole_rates):
-    full_grad = lax.all_gather(out_grad, "grp", axis=1, tiled=True)
+    full_grad = connect_forms_here(out_grad)
     length = full_grad.shape[0]
     col_width = out_grad.shape[1]
     poles = pole_rates.shape[0]

time: 492 us -> 459 us (0.933)
  waiting for transfers between devices: 236 us -> 195 us
  local copies, waits for them, and re-layouts: 4.96 us -> 12.1 us
    all_gather x1, waiting for transfers between devices: 143 us -> 105 us  [per_device(): lax.all_gather(filter_mats, 'ctx', axis=1, tiled=True)]
    all_gather x1 -> x0, waiting for transfers between devices: 27.7 us -> none  [per_device(): full_grad = lax.all_gather(out_grad, 'grp', axis=1, tiled=True)]
    all_to_all x0 -> x1, waiting for transfers between devices: none -> 24.8 us  [link_the_slabs(): jax.lax.all_to_all(jnp.stack([field_in] * jax.lax.axis_size('grp')), 'grp...]
    reshape x0 -> x2, local copies, waits for them, and re-layouts: none -> 5.4 us  [link_the_slabs(): jnp.concatenate(jax.lax.all_to_all(jnp.stack([field_in] * jax.lax.axis_si...]
  transfers between devices with their start and end apart: 5 -> 5, of which waited for: 3 -> 3; matrix products, arithmetic and copies ran while one was open for 13% -> 15% of each run, Pallas kernels for 0% -> 0%
where the time goes in v2:
time: 459 us; the launch traced here: 458 us
  waiting for transfers between devices  195 us (42%)
  blocking collectives  148 us (32%)
  matrix products  43.2 us (9%)
  other arithmetic  41.2 us (9%)
  between operations  13.9 us (3%)
  local copies, waits for them, and re-layouts  12.1 us (3%)
    unnamed x1, blocking collectives  148 us
    all_gather x1, waiting for transfers between devices, per_device(): lax.all_gather(filter_mats, 'ctx', axis=1, tiled=True)  105 us
    psum x1, waiting for transfers between devices, per_device(): pole_sum = lax.psum(stacked[length:], 'grp')  63.9 us
    select_n x32, other arithmetic, step(): return jax.tree.map(lambda a, b: jnp.where(reached, a, b), new, before)  39.8 us
    all_to_all x1, waiting for transfers between devices, link_the_slabs(): jax.lax.all_to_all(jnp.stack([field_in] * jax.lax.axis_size('grp')), 'grp...  24.8 us
    dot_general x1, matrix products, per_device(): jnp.einsum('kts,kti->si', kernel_mat, proj_grad, precision=exact_prec)  17.5 us
    dot_general x1, matrix products, per_device(): jnp.einsum('tj,kij->kti', full_grad, lax.all_gather(filter_mats, 'ctx', a...  12.2 us
  transfers between devices with their start and end apart: 5, of which 3 were waited for; matrix products, arithmetic and copies ran while one was open for 15% of the time, Pallas kernels for 0%

profile of v2, /device:TPU:0, one launch (start us, length us, event | category | flops | bytes accessed | tf_op | source)
XLA Modules:
  0.0 457.7 jit_solution(398114570787341983)
XLA Ops:
  7.3 2.4 stack.2
  9.7 3.6 all-to-all-start
  15.5 24.8 %all-to-all-done = bf16[8,512,256]{2,1,0:T(8,128)(2,1)S(1)} async-done(((bf16[8,512,256]{2,1,0:T(8,128)(2,1)}), bf16[8,512,256]{2,1,0:T(8,128)(2,1)S(1)}, u32[]{:S(2)}, u32[]{:S(2)}) %all-to-all-start) | async-done | bytes 2097184 | tf_op jit(solution)/shard_map/all_to_all | solution.py:12
  40.4 2.5 copy.9
  42.9 2.9 reshape.77
  45.8 105.1 %all-gather.4.cloned.1.call-done = bf16[2,2048,2048]{2,1,0:T(8,128)(2,1)} async-done(((bf16[2,64,2048]{2,1,0:T(8,128)(2,1)}), bf16[2,2048,2048]{2,1,0:T(8,128)(2,1)}) %all-gather.4.cloned.1.call-update) | async-done | bytes 16777232 | tf_op jit(solution)/shard_map/all_gather | solution.py:69
  150.9 12.2 %fusion.35 = f32[2,2048,512]{2,1,0:T(8,128)S(1)} fusion(bf16[2,2048,2048]{2,1,0:T(8,128)(2,1)} %all-gather.4.cloned.1.call-done, bf16[512,2048,1]{1,0,2:T(8,128)(2,1)S(1)} %reshape.77), kind=kOutput, calls=%fused_computation.45 | convolution fusion | flops 8589934592 | bytes 27262976 | tf_op jit(solution)/shard_map/tj,kij->kti/dot_general | solution.py:66
  163.1 3.3 copy-done
  166.3 9.1 %fusion.8 = f32[1,80,2048]{2,1,0:T(8,128)} fusion(f32[2,2048,512]{2,1,0:T(8,128)S(1)} %fusion.35, f32[80,512]{1,0:T(8,128)S(1)} %multiply_exponential_fusion, f32[2,80]{1,0:T(2,128)S(1)} %get-tuple-element.167), kind=kOutput, calls=%fused_computation.8 | convolution fusion | flops 2013347840 | bytes 9208448 | tf_op jit(solution)/shard_map/kpt,kti->pi/dot_general | solution.py:73
  175.5 63.9 %all-reduce.3.cloned.1.call-done = f32[1,80,2048]{2,1,0:T(8,128)} async-done(((f32[1,80,2048]{2,1,0:T(8,128)}), f32[1,80,2048]{2,1,0:T(8,128)}) %all-reduce.3.cloned.1.call-update) | async-done | bytes 655376 | tf_op jit(solution)/shard_map/psum | solution.py:76
  239.6 147.6 %all-reduce = f32[2560]{0:T(1024)S(1)} all-reduce(f32[2560]{0:T(1024)S(1)} %get-tuple-element.168), channel_id=2, replica_groups=mesh['ctx'=32,'grp'=8] {'ctx'}, use_global_device_ids=true, to_apply=%add | all-reduce | flops 2560 | bytes 20480
  387.8 1.9 fusion.15
  389.7 17.5 %fusion.5 = f32[512,2048]{1,0:T(8,128)} fusion(f32[2,2048,512]{2,1,0:T(8,128)} %copy-done, f32[2,512,512]{1,2,0:T(8,128)S(1)} %fusion.15, pred[512,512]{0,1:T(8,128)(4,1)S(1)} %iota_compare_fusion), kind=kOutput, calls=%fused_computation.7 | convolution fusion | flops 12885426176 | bytes 14942208 | tf_op jit(solution)/shard_map/kts,kti->si/dot_general | solution.py:72
  407.3 41.4 %while.16 = (s32[]{:T(128)}, f32[80,2048]{1,0:T(8,128)S(1)}, s32[]{:T(128)}, f32[32,80,2048]{2,1,0:T(8,128)}, f32[32,80,1]{1,2,0:T(1,128)S(1)}, /*index=5*/s32[]{:T(128)}, s32[]{:T(128)}, s32[]{:T(128)}, s32[]{:T(128)}) while((s32[]{:T(128)}, f32[80,2048]{1,0:T(8,128)S(1)}, s32[]{:T(128)}, f32[32,80,2048]{2,1,0:T(8,128)}, ...), condition=%wide.region_3.4_spmd.clone, body=%wide.region_2.3_spmd.clone.sunk | while | flops 655368 | bytes 1967215 | solution.py:35
  413.8 1.3 fusion.39
  417.7 1.2 fusion.39
  419.0 1.3 fusion.39
  420.3 1.2 fusion.39
  421.6 1.2 fusion.39
  422.9 1.3 fusion.39
  425.4 1.2 fusion.39
  426.7 1.2 fusion.39
  428.0 1.3 fusion.39
  429.3 1.3 fusion.39
  430.6 1.2 fusion.39
  433.2 1.3 fusion.39
  434.5 1.3 fusion.39
  435.8 1.2 fusion.39
  437.1 1.2 fusion.39
  441.0 1.2 fusion.39
  442.3 1.2 fusion.39
  448.7 2.5 fusion.12
  (77 shorter events, 21.9 us)
Async XLA Ops:
  6.5 6.8 %copy-start.2 = (u32[256]{0:T(256)S(1)}, u32[256]{0:T(256)}, u32[]{:S(2)}) copy-start(u32[256]{0:T(256)} %constant.76) | copy-start | bytes 3076
  6.5 8.1 %copy-start.1 = (f32[80]{0:T(128)S(1)}, f32[80]{0:T(128)}, u32[]{:S(2)}) copy-start(f32[80]{0:T(128)} %param.9) | copy-start | bytes 964
  6.5 144.3 %all-gather.4.cloned.1.call-start = ((), (), s32[]{:S(2)}) async-start(), calls=%async_computation.2 | async-start | bytes 17301504 | tf_op jit(solution)/shard_map/all_gather | solution.py:69
  9.7 30.7 %all-to-all-start = ((bf16[8,512,256]{2,1,0:T(8,128)(2,1)}), bf16[8,512,256]{2,1,0:T(8,128)(2,1)S(1)}, u32[]{:S(2)}, u32[]{:S(2)}) async-start(bf16[8,512,256]{2,1,0:T(8,128)(2,1)} %stack.2), calls=%async_computation | async-start | bytes 4194304 | tf_op jit(solution)/shard_map/all_to_all | solution.py:12
  13.3 226.1 %all-reduce.3.cloned.1.call-start = ((), (), s32[]{:S(2)}) async-start(), calls=%async_computation.4 | async-start | bytes 1310720 | tf_op jit(solution)/shard_map/psum | solution.py:76
  163.1 3.3 copy-start
  175.5 231.8 %all-gather.6.cloned.1.call-start = ((), (), s32[]{:S(2)}) async-start(), calls=%async_computation.5 | async-start | bytes 21626880 | tf_op jit(solution)/shard_map/all_gather | solution.py:22
  239.4 209.3 %reduce-scatter.2.cloned.1.call-start = ((), (), s32[]{:S(2)}) async-start(), calls=%async_computation.3 | async-start | bytes 4718592 | tf_op jit(solution)/shard_map/reduce_scatter | solution.py:75
Sparse Core Ops, SparseCore 0:
  9.9 140.8 all-gather.3
  175.6 63.7 all-reduce.2
  242.0 161.0 all-gather.5
  407.4 35.4 reduce-scatter.1
